TPU v7x, 512 devices: a whole 4x4x16 slice. The times are simulated.
512 devices in a mesh: seq: 64 (over z, x), head: 8 (over y, core).
Axes of the slice: x: 4, y: 4, z: 16, core: 2. Of those that a mesh axis runs over, the one named last changes fastest.
Arguments:
- activations: bfloat16 [32768, 2048], P('seq', 'head'), may hold values from -6 to 6
- w_proj: bfloat16 [3, 2048, 2048], P(None, None, 'head'), may hold values from -0.125 to 0.125
- level_weight: float32 [32768, 16, 16], P('seq', 'head'), may hold values from 0.25 to 4
- grad_out: bfloat16 [32768, 2048], P('seq', 'head'), may hold values from -6 to 6
Outputs:
- attn_output: bfloat16 [32768, 2048], P('seq', 'head')
- grad_query: bfloat16 [32768, 2048], P('seq', 'head')
- grad_key: bfloat16 [32768, 2048], P('seq', 'head')
- grad_value: bfloat16 [32768, 2048], P('seq', 'head')
All inputs are finite; a program needn't handle non-finite values.
Results may differ from a plain program's by a relative error of at most 0.0085.
Values may be sent and summed in bfloat16 or wider, within the bound.
No kernel may reach another device: no remote copies, remote signals or barrier semaphores. Data moves between devices by JAX's collectives and lax.ppermute only.
A program may use at most 64 MiB of HBM per device.

v0:
```python
import jax
import jax.numpy as jnp
from jax import lax
from jax.sharding import PartitionSpec as P


def sent_to_all(value, axis):
    peers = lax.axis_size(axis)
    return lax.all_to_all(
        jnp.broadcast_to(value[None], (peers, *value.shape)), axis, 0, 0, tiled=True
    )


def joined_along(tiles, dim):
    tiles = jnp.moveaxis(tiles, 0, dim)
    shape = tiles.shape
    return tiles.reshape(*shape[:dim], shape[dim] * shape[dim + 1], *shape[dim + 2 :])


def gathered_copies(value, axis, dim):
    tiles = sent_to_all(value, axis)
    return joined_along(tiles, dim)


def partner_2(value, axis, bit):
    return lax.ppermute(value, axis, [(i, i ^ 1 << bit) for i in range(lax.axis_size(axis))])


def bit_length_of(numbers, width):
    total = jnp.zeros_like(numbers)
    for shift_by in range(width):
        total = total + (jnp.right_shift(numbers, shift_by) > 0).astype(jnp.int32)
    return total


def level_factors(count):
    index_list = jnp.arange(count, dtype=jnp.int32)
    return jnp.exp2(-0.5 * (jnp.maximum(index_list, 1) - 1).astype(jnp.float32))


def on_device(activations, w_proj, level_weight, grad_out):
    highest = lax.Precision.HIGHEST
    block_len = activations.shape[0]
    local_width = w_proj.shape[2]
    head_count = level_weight.shape[1]
    head_dim = local_width // head_count
    scale = head_dim ** (-0.5)
    block_bits = block_len.bit_length() - 1
    seq_bits = lax.axis_size("seq").bit_length() - 1
    seq_index = lax.axis_index("seq")
    projected = jnp.einsum(
        "tn,cnf->tcf",
        gathered_copies(activations, "head", 1),
        w_proj,
        preferred_element_type=jnp.float32,
    )
    projected = projected.astype(jnp.bfloat16).reshape(block_len, 3, head_count, head_dim)
    query_rows = projected[:, 0]
    key_rows = projected[:, 1]
    value_rows = projected[:, 2]
    cotangent = grad_out.reshape(block_len, head_count, head_dim)
    weight = level_weight * level_factors(level_weight.shape[2])
    local_pos = jnp.arange(block_len, dtype=jnp.int32)
    local_level = bit_length_of(jnp.bitwise_xor(local_pos[:, None], local_pos[None, :]), block_bits)
    causal = local_pos[None, :] <= local_pos[:, None]
    mask_weight = jnp.zeros((head_count, block_len, block_len), jnp.float32)
    for level_ix in range(block_bits + 1):
        chosen = (local_level == level_ix) & causal
        mask_weight = mask_weight + jnp.where(
            chosen[None], weight[:, :, level_ix].T[:, :, None], 0.0
        )
    scores = (
        jnp.einsum("thd,shd->hts", query_rows, key_rows, preferred_element_type=jnp.float32) * scale
    )
    attn = (scores * mask_weight).astype(jnp.bfloat16)
    out_inner = jnp.einsum("hts,shd->thd", attn, value_rows, preferred_element_type=jnp.float32)
    back = jnp.einsum("thd,shd->hts", cotangent, value_rows, preferred_element_type=jnp.float32)
    grads = (back * mask_weight * scale).astype(jnp.bfloat16)
    dq_inner = jnp.einsum("hts,shd->thd", grads, key_rows, preferred_element_type=jnp.float32)
    dk_inner = jnp.einsum("hts,thd->shd", grads, query_rows, preferred_element_type=jnp.float32)
    dv_inner = jnp.einsum("hts,thd->shd", attn, cotangent, preferred_element_type=jnp.float32)
    cross = weight[:, :, block_bits + 1 :]
    states = jnp.einsum("shx,shy->hxy", key_rows, value_rows, preferred_element_type=jnp.float32)
    weighted = cross[:, :, :, None] * query_rows.astype(jnp.float32)[:, :, None, :]
    level_grads = jnp.einsum(
        "thjx,thy->jhxy", weighted, cotangent.astype(jnp.float32), precision=highest
    )
    bit_flags = [
        (jnp.right_shift(seq_index, bit_index) % 2).astype(jnp.float32)
        for bit_index in range(seq_bits)
    ]
    upward = []
    prefix = None
    lead = 1
    moving = jnp.concatenate([states[None], level_grads], 0)
    downward = []
    for bit_index in range(seq_bits):
        partner = partner_2(moving.astype(jnp.bfloat16), "seq", bit_index).astype(moving.dtype)
        upward.append(partner[0] * bit_flags[bit_index])
        downward.append(partner[lead] * (1.0 - bit_flags[bit_index]))
        summed = moving + partner
        moving = jnp.concatenate([summed[:lead], summed[lead + 1 :]], 0)
    prefix = jnp.stack(upward)
    prefix_half = prefix.astype(jnp.bfloat16)
    suffix_half = jnp.stack(downward).astype(jnp.bfloat16)
    reads = jnp.einsum(
        "thx,jhxy->thjy", query_rows, prefix_half, preferred_element_type=jnp.float32
    )
    out_cross = scale * jnp.sum(cross[..., None] * reads, 2)
    reads_back = jnp.einsum(
        "thy,jhxy->thjx", cotangent, prefix_half, preferred_element_type=jnp.float32
    )
    dq_cross = scale * jnp.sum(cross[..., None] * reads_back, 2)
    dk_cross = scale * jnp.einsum(
        "shy,jhxy->shx", value_rows, suffix_half, preferred_element_type=jnp.float32
    )
    dv_cross = scale * jnp.einsum(
        "shx,jhxy->shy", key_rows, suffix_half, preferred_element_type=jnp.float32
    )

    def finish(total):
        return total.reshape(block_len, local_width).astype(jnp.bfloat16)

    return (
        finish(out_inner + out_cross),
        finish(dq_inner + dq_cross),
        finish(dk_inner + dk_cross),
        finish(dv_inner + dv_cross),
    )


def solution(mesh):
    in_specs = (P("seq", "head"), P(None, None, "head"), P("seq", "head", None), P("seq", "head"))
    out_specs = (P("seq", "head"), P("seq", "head"), P("seq", "head"), P("seq", "head"))
    return jax.shard_map(
        on_device, mesh=mesh, in_specs=in_specs, out_specs=out_specs, check_vma=False
    )
```

profile of v0, /device:TPU:1, one launch (start us, length us, event | category | flops | bytes accessed | tf_op | source)
XLA Modules:
  0.0 170.6 jit_solution(4373470797296666263)
XLA Ops:
  0.6 2.6 %broadcast_in_dim.157 = bf16[8,512,256]{2,1,0:T(8,128)(2,1)} broadcast(bf16[512,256]{1,0:T(8,128)(2,1)} %param.4), dimensions={1,2} | broadcast | bytes 2359296 | tf_op jit(solution)/shard_map/broadcast_in_dim | solution.py:10
  3.2 11.2 %all-to-all-start = ((bf16[8,512,256]{2,1,0:T(8,128)(2,1)}), bf16[8,512,256]{2,1,0:T(8,128)(2,1)}, u32[]{:S(2)}, u32[]{:S(2)}) async-start(bf16[8,512,256]{2,1,0:T(8,128)(2,1)} %broadcast_in_dim.157), calls=%async_computation | async-start | bytes 4194304 | tf_op jit(solution)/shard_map/all_to_all | solution.py:9
  14.6 0.6 slice.159
  15.2 1.0 reshape.293
  16.3 0.9 copy.69
  17.1 0.6 copy_bitcast_fusion.2
  17.7 0.6 copy_bitcast_fusion.4
  18.3 0.6 copy_bitcast_fusion.6
  18.9 1.8 %fusion.19 = (pred[512,512]{1,0:T(8,128)(4,1)}, pred[512,512]{1,0:T(8,128)(4,1)}) fusion(), kind=kLoop, calls=%fused_computation.31 | loop fusion | flops 10747904 | bytes 524288 | tf_op jit(solution)/shard_map/and | solution.py:68
  20.8 1.8 %fusion.21 = (pred[512,512]{1,0:T(8,128)(4,1)}, pred[512,512]{1,0:T(8,128)(4,1)}) fusion(), kind=kLoop, calls=%fused_computation.33 | loop fusion | flops 10747904 | bytes 524288 | tf_op jit(solution)/shard_map/and | solution.py:68
  22.6 1.8 %fusion.23 = (pred[512,512]{1,0:T(8,128)(4,1)}, pred[512,512]{1,0:T(8,128)(4,1)}) fusion(), kind=kLoop, calls=%fused_computation.35 | loop fusion | flops 10747904 | bytes 524288 | tf_op jit(solution)/shard_map/and | solution.py:68
  24.4 1.8 %fusion.25 = (pred[512,512]{1,0:T(8,128)(4,1)}, pred[512,512]{1,0:T(8,128)(4,1)}) fusion(), kind=kLoop, calls=%fused_computation.37 | loop fusion | flops 10747904 | bytes 524288 | tf_op jit(solution)/shard_map/and | solution.py:68
  26.2 14.6 %all-to-all-done = bf16[8,512,256]{2,1,0:T(8,128)(2,1)} async-done(((bf16[8,512,256]{2,1,0:T(8,128)(2,1)}), bf16[8,512,256]{2,1,0:T(8,128)(2,1)}, u32[]{:S(2)}, u32[]{:S(2)}) %all-to-all-start) | async-done | bytes 2097184 | tf_op jit(solution)/shard_map/all_to_all | solution.py:9
  40.8 4.1 %copy.52 = bf16[512,8,256]{2,1,0:T(8,128)(2,1)} copy(bf16[512,8,256]{2,0,1:T(8,128)(2,1)} %bitcast) | data formatting | bytes 4194304 | tf_op jit(solution)/shard_map/transpose | solution.py:15
  44.9 4.2 %reshape.294 = bf16[512,2048,1]{1,0,2:T(8,128)(2,1)} reshape(bf16[512,8,256]{2,1,0:T(8,128)(2,1)} %copy.52) | data formatting | bytes 4194304 | tf_op jit(solution)/shard_map/reshape | solution.py:17
  49.1 3.4 %convolution_convert_fusion = bf16[512,3,256]{0,2,1:T(8,128)(2,1)S(1)} fusion(bf16[512,2048,1]{1,0,2:T(8,128)(2,1)} %reshape.294, bf16[3,2048,256]{2,1,0:T(8,128)(2,1)S(1)} %copy-done), kind=kOutput, calls=%fused_computation.13 | convolution fusion | flops 1611005952 | bytes 6029312 | tf_op jit(solution)/shard_map/tn,cnf->tcf/dot_general | solution.py:51
  52.5 0.8 slice.147
  53.7 1.1 copy.102
  54.8 0.8 bitcast_convert_fusion
  55.7 2.1 %copy.58 = f32[512,2,128]{0,2,1:T(8,128)} copy(f32[512,2,128]{2,0,1:T(8,128)} %bitcast_convert_fusion) | data formatting | bytes 1048576 | tf_op jit(solution)/shard_map/convert_element_type | solution.py:84
  57.7 2.7 %fusion.8 = f32[6,2,128,128]{3,2,0,1:T(8,128)S(1)} fusion(f32[512,2,128]{0,2,1:T(8,128)} %copy.58, f32[512,2,6]{0,2,1:T(8,128)} %slice.159, bf16[512,2,128,1]{2,1,0,3:T(2,128)(2,1)} %bitcast.142), kind=kOutput, calls=%fused_computation.14 | convolution fusion | flops 1208745984 | bytes 1597440 | tf_op jit(solution)/shard_map/thjx,thy->jhxy/dot_general | solution.py:85
  60.5 2.1 %collective-permute-start = (bf16[7,2,128,128]{3,2,0,1:T(8,128)(2,1)S(1)}, bf16[7,2,128,128]{3,2,0,1:T(8,128)(2,1)S(1)}, u32[]{:S(2)}, u32[]{:S(2)}) collective-permute-start(bf16[7,2,128,128]{3,2,0,1:T(8,128)(2,1)S(1)} %fusion.30), channel_id=1, source_target_pairs={{0,8},{8,0},{16,24},{24,16},{32,40},{40,32},{48,56},{56,48},{64,72... | collective-permute-start | bytes 1376264 | tf_op jit(solution)/shard_map/ppermute | solution.py:26
  62.7 1.0 fusion.27
  63.8 9.7 %collective-permute-done = bf16[7,2,128,128]{3,2,0,1:T(8,128)(2,1)S(1)} collective-permute-done((bf16[7,2,128,128]{3,2,0,1:T(8,128)(2,1)S(1)}, bf16[7,2,128,128]{3,2,0,1:T(8,128)(2,1)S(1)}, u32[]{:S(2)}, u32[]{:S(2)}) %collective-permute-start) | collective-permute-done | bytes 458784 | tf_op jit(solution)/shard_map/ppermute | solution.py:26
  73.8 1.9 %collective-permute-start.1 = (bf16[6,2,128,128]{3,2,0,1:T(8,128)(2,1)S(1)}, bf16[6,2,128,128]{3,2,0,1:T(8,128)(2,1)S(1)}, u32[]{:S(2)}, u32[]{:S(2)}) collective-permute-start(bf16[6,2,128,128]{3,2,0,1:T(8,128)(2,1)S(1)} %fusion.32), channel_id=1, source_target_pairs={{0,16},{8,24},{16,0},{24,8},{32,48},{40,56},{48,32},{56,40},{64,80... | collective-permute-start | bytes 1179656 | tf_op jit(solution)/shard_map/ppermute | solution.py:26
  75.9 3.4 %multiply_convert_fusion = bf16[2,512,512]{2,1,0:T(8,128)(2,1)S(1)} fusion(bf16[512,3,2,128]{0,3,2,1:T(8,128)(2,1)S(1)} %bitcast.137, f32[2,512]{1,0:T(2,128)S(1)} %get-tuple-element.40, pred[512,512]{1,0:T(8,128)(4,1)S(1)} %copy-done.7, f32[2,512]{1,0:T(2,128)S(1)} %get-tuple-element.41, pred[512,512]{1,0:T(8,128)(4,1)S(1)} %copy-done.8, ...), kind=kOutput, calls=%fused_computation.9 | convolution fusion | flops 145752064 | bytes 4235264 | tf_op jit(solution)/shard_map/thd,shd->hts/dot_general | solution.py:73
  79.3 6.7 %collective-permute-done.1 = bf16[6,2,128,128]{3,2,0,1:T(8,128)(2,1)S(1)} collective-permute-done((bf16[6,2,128,128]{3,2,0,1:T(8,128)(2,1)S(1)}, bf16[6,2,128,128]{3,2,0,1:T(8,128)(2,1)S(1)}, u32[]{:S(2)}, u32[]{:S(2)}) %collective-permute-start.1) | collective-permute-done | bytes 393248 | tf_op jit(solution)/shard_map/ppermute | solution.py:26
  86.2 1.9 %collective-permute-start.2 = (bf16[5,2,128,128]{3,2,0,1:T(8,128)(2,1)S(1)}, bf16[5,2,128,128]{3,2,0,1:T(8,128)(2,1)S(1)}, u32[]{:S(2)}, u32[]{:S(2)}) collective-permute-start(bf16[5,2,128,128]{3,2,0,1:T(8,128)(2,1)S(1)} %fusion.34), channel_id=1, source_target_pairs={{0,32},{8,40},{16,48},{24,56},{32,0},{40,8},{48,16},{56,24},{64,96... | collective-permute-start | bytes 983048 | tf_op jit(solution)/shard_map/ppermute | solution.py:26
  88.2 4.1 %fusion.5 = bf16[2,512,512]{2,1,0:T(8,128)(2,1)} fusion(bf16[512,2,128]{0,2,1:T(8,128)(2,1)S(1)} %copy-done.6, bf16[512,3,2,128]{0,3,2,1:T(8,128)(2,1)S(1)} %bitcast.138, f32[2,512]{1,0:T(2,128)S(1)} %get-tuple-element.40, pred[512,512]{1,0:T(8,128)(4,1)S(1)} %copy-done.7, f32[2,512]{1,0:T(2,128)S(1)} %get-tuple-element.41, ...), kind=kOutput, calls=%fused_computation.8 | convolution fusion | flops 145752064 | bytes 4235264 | tf_op jit(solution)/shard_map/thd,shd->hts/dot_general | solution.py:77
  92.5 2.2 %collective-permute-done.2 = bf16[5,2,128,128]{3,2,0,1:T(8,128)(2,1)S(1)} collective-permute-done((bf16[5,2,128,128]{3,2,0,1:T(8,128)(2,1)S(1)}, bf16[5,2,128,128]{3,2,0,1:T(8,128)(2,1)S(1)}, u32[]{:S(2)}, u32[]{:S(2)}) %collective-permute-start.2) | collective-permute-done | bytes 327712 | tf_op jit(solution)/shard_map/ppermute | solution.py:26
  94.9 1.9 %collective-permute-start.3 = (bf16[4,2,128,128]{3,2,0,1:T(8,128)(2,1)S(1)}, bf16[4,2,128,128]{3,2,0,1:T(8,128)(2,1)S(1)}, u32[]{:S(2)}, u32[]{:S(2)}) collective-permute-start(bf16[4,2,128,128]{3,2,0,1:T(8,128)(2,1)S(1)} %fusion.36), channel_id=1, source_target_pairs={{0,64},{8,72},{16,80},{24,88},{32,96},{40,104},{48,112},{56,120},{... | collective-permute-start | bytes 786440 | tf_op jit(solution)/shard_map/ppermute | solution.py:26
  97.0 13.6 %collective-permute-done.3 = bf16[4,2,128,128]{3,2,0,1:T(8,128)(2,1)S(1)} collective-permute-done((bf16[4,2,128,128]{3,2,0,1:T(8,128)(2,1)S(1)}, bf16[4,2,128,128]{3,2,0,1:T(8,128)(2,1)S(1)}, u32[]{:S(2)}, u32[]{:S(2)}) %collective-permute-start.3) | collective-permute-done | bytes 262176 | tf_op jit(solution)/shard_map/ppermute | solution.py:26
  110.8 4.6 %collective-permute-start.4 = (bf16[3,2,128,128]{3,2,0,1:T(8,128)(2,1)S(1)}, bf16[3,2,128,128]{3,2,0,1:T(8,128)(2,1)S(1)}, u32[]{:S(2)}, u32[]{:S(2)}) collective-permute-start(bf16[3,2,128,128]{3,2,0,1:T(8,128)(2,1)S(1)} %fusion.37), channel_id=1, source_target_pairs={{0,128},{8,136},{16,144},{24,152},{32,160},{40,168},{48,176},{56,1... | collective-permute-start | bytes 589832 | tf_op jit(solution)/shard_map/ppermute | solution.py:26
  115.4 18.0 %collective-permute-done.4 = bf16[3,2,128,128]{3,2,0,1:T(8,128)(2,1)S(1)} collective-permute-done((bf16[3,2,128,128]{3,2,0,1:T(8,128)(2,1)S(1)}, bf16[3,2,128,128]{3,2,0,1:T(8,128)(2,1)S(1)}, u32[]{:S(2)}, u32[]{:S(2)}) %collective-permute-start.4) | collective-permute-done | bytes 196640 | tf_op jit(solution)/shard_map/ppermute | solution.py:26
  133.6 11.3 %collective-permute-start.5 = (bf16[2,2,128,128]{3,2,0,1:T(8,128)(2,1)S(1)}, bf16[2,2,128,128]{3,2,0,1:T(8,128)(2,1)S(1)}, u32[]{:S(2)}, u32[]{:S(2)}) collective-permute-start(bf16[2,2,128,128]{3,2,0,1:T(8,128)(2,1)S(1)} %pad_maximum_fusion.5), channel_id=1, source_target_pairs={{0,256},{8,264},{16,272},{24,280},{32,288},{40,296},{48,304},{56,3... | collective-permute-start | bytes 393224 | tf_op jit(solution)/shard_map/ppermute | solution.py:26
  145.0 12.2 %collective-permute-done.5 = bf16[2,2,128,128]{3,2,0,1:T(8,128)(2,1)S(1)} collective-permute-done((bf16[2,2,128,128]{3,2,0,1:T(8,128)(2,1)S(1)}, bf16[2,2,128,128]{3,2,0,1:T(8,128)(2,1)S(1)}, u32[]{:S(2)}, u32[]{:S(2)}) %collective-permute-start.5) | collective-permute-done | bytes 131104 | tf_op jit(solution)/shard_map/ppermute | solution.py:26
  157.3 0.3 fusion.14
  157.6 1.0 convolution_multiply_fusion.1
  158.6 1.4 fusion
  159.9 1.4 fusion.1
  161.4 0.3 fusion.17
  161.7 0.8 copy.74
  162.5 1.7 %fusion.18 = bf16[2,128,512]{2,1,0:T(8,128)(2,1)S(1)} fusion(f32[2,128,512]{2,1,0:T(8,128)} %convolution_multiply_fusion.1, bf16[2,512,512]{2,1,0:T(8,128)(2,1)} %fusion.5, bf16[512,3,2,128]{0,3,2,1:T(8,128)(2,1)} %bitcast.134), kind=kOutput, calls=%fused_computation.28 | convolution fusion | flops 134479872 | bytes 2097152 | tf_op jit(solution)/shard_map/hts,thd->shd/dot_general | solution.py:80
  164.3 0.8 copy.73
  165.1 1.9 %fusion.16 = bf16[512,2,128]{0,2,1:T(8,128)(2,1)S(1)} fusion(bf16[2,512,512]{2,1,0:T(8,128)(2,1)} %fusion.5, f32[512,2,128]{0,2,1:T(8,128)} %fusion, bf16[512,3,2,128]{0,3,2,1:T(8,128)(2,1)} %bitcast.135), kind=kOutput, calls=%fused_computation.26 | convolution fusion | flops 134610944 | bytes 2097152 | tf_op jit(solution)/shard_map/hts,shd->thd/dot_general | solution.py:79
  167.0 0.8 copy.72
  167.9 1.9 %fusion.15 = bf16[512,2,128]{0,2,1:T(8,128)(2,1)S(1)} fusion(bf16[2,512,512]{2,1,0:T(8,128)(2,1)} %copy-done.1, f32[512,2,128]{0,2,1:T(8,128)} %fusion.1, bf16[512,3,2,128]{0,3,2,1:T(8,128)(2,1)} %bitcast.136), kind=kOutput, calls=%fused_computation.25 | convolution fusion | flops 134610944 | bytes 2097152 | tf_op jit(solution)/shard_map/hts,shd->thd/dot_general | solution.py:76
  169.8 0.8 copy.71
  (85 shorter events, 2.0 us)
Async XLA Ops:
  0.6 48.5 %copy-start = (bf16[3,2048,256]{2,1,0:T(8,128)(2,1)S(1)}, bf16[3,2048,256]{2,1,0:T(8,128)(2,1)}, u32[]{:S(2)}) copy-start(bf16[3,2048,256]{2,1,0:T(8,128)(2,1)} %param.5) | copy-start | bytes 9437188
  3.2 11.2 %copy-start.15 = (f32[512,2,16]{0,2,1:T(8,128)S(1)}, f32[512,2,16]{0,2,1:T(8,128)}, u32[]{:S(2)}) copy-start(f32[512,2,16]{0,2,1:T(8,128)} %param.6) | copy-start | bytes 196612
  3.2 37.5 %all-to-all-start = ((bf16[8,512,256]{2,1,0:T(8,128)(2,1)}), bf16[8,512,256]{2,1,0:T(8,128)(2,1)}, u32[]{:S(2)}, u32[]{:S(2)}) async-start(bf16[8,512,256]{2,1,0:T(8,128)(2,1)} %broadcast_in_dim.157), calls=%async_computation | async-start | bytes 4194304 | tf_op jit(solution)/shard_map/all_to_all | solution.py:9
  16.2 28.7 %copy-start.4 = (bf16[512,2,128]{2,1,0:T(2,128)(2,1)}, bf16[512,2,128]{2,1,0:T(2,128)(2,1)S(1)}, u32[]{:S(2)}) copy-start(bf16[512,2,128]{2,1,0:T(2,128)(2,1)S(1)} %reshape.293) | copy-start | bytes 786436
  52.5 1.0 copy-start.2
  60.5 13.0 %collective-permute-start = (bf16[7,2,128,128]{3,2,0,1:T(8,128)(2,1)S(1)}, bf16[7,2,128,128]{3,2,0,1:T(8,128)(2,1)S(1)}, u32[]{:S(2)}, u32[]{:S(2)}) collective-permute-start(bf16[7,2,128,128]{3,2,0,1:T(8,128)(2,1)S(1)} %fusion.30), channel_id=1, source_target_pairs={{0,8},{8,0},{16,24},{24,16},{32,40},{40,32},{48,56},{56,48},{64,72... | collective-permute-start | bytes 1376264 | tf_op jit(solution)/shard_map/ppermute | solution.py:26
  63.7 12.0 %copy-start.3 = (bf16[512,3,256]{0,2,1:T(8,128)(2,1)S(1)}, bf16[512,3,256]{0,2,1:T(8,128)(2,1)}, u32[]{:S(2)}) copy-start(bf16[512,3,256]{0,2,1:T(8,128)(2,1)} %copy-done.2) | copy-start | bytes 2359300
  63.7 12.0 %copy-start.7 = (pred[512,512]{1,0:T(8,128)(4,1)S(1)}, pred[512,512]{1,0:T(8,128)(4,1)}, u32[]{:S(2)}) copy-start(pred[512,512]{1,0:T(8,128)(4,1)} %get-tuple-element.50) | copy-start | bytes 786436
  63.7 12.0 %copy-start.8 = (pred[512,512]{1,0:T(8,128)(4,1)S(1)}, pred[512,512]{1,0:T(8,128)(4,1)}, u32[]{:S(2)}) copy-start(pred[512,512]{1,0:T(8,128)(4,1)} %get-tuple-element.51) | copy-start | bytes 786436
  63.7 12.0 %copy-start.9 = (pred[512,512]{1,0:T(8,128)(4,1)S(1)}, pred[512,512]{1,0:T(8,128)(4,1)}, u32[]{:S(2)}) copy-start(pred[512,512]{1,0:T(8,128)(4,1)} %get-tuple-element.52) | copy-start | bytes 786436
  63.7 12.0 %copy-start.10 = (pred[512,512]{1,0:T(8,128)(4,1)S(1)}, pred[512,512]{1,0:T(8,128)(4,1)}, u32[]{:S(2)}) copy-start(pred[512,512]{1,0:T(8,128)(4,1)} %get-tuple-element.53) | copy-start | bytes 786436
  63.7 12.0 %copy-start.11 = (pred[512,512]{1,0:T(8,128)(4,1)S(1)}, pred[512,512]{1,0:T(8,128)(4,1)}, u32[]{:S(2)}) copy-start(pred[512,512]{1,0:T(8,128)(4,1)} %get-tuple-element.54) | copy-start | bytes 786436
  63.8 12.0 %copy-start.12 = (pred[512,512]{1,0:T(8,128)(4,1)S(1)}, pred[512,512]{1,0:T(8,128)(4,1)}, u32[]{:S(2)}) copy-start(pred[512,512]{1,0:T(8,128)(4,1)} %get-tuple-element.55) | copy-start | bytes 786436
  63.8 12.0 %copy-start.13 = (pred[512,512]{1,0:T(8,128)(4,1)S(1)}, pred[512,512]{1,0:T(8,128)(4,1)}, u32[]{:S(2)}) copy-start(pred[512,512]{1,0:T(8,128)(4,1)} %get-tuple-element.56) | copy-start | bytes 786436
  63.8 12.0 %copy-start.14 = (pred[512,512]{1,0:T(8,128)(4,1)S(1)}, pred[512,512]{1,0:T(8,128)(4,1)}, u32[]{:S(2)}) copy-start(pred[512,512]{1,0:T(8,128)(4,1)} %get-tuple-element.57) | copy-start | bytes 786436
  63.8 12.0 %copy-start.17 = (f32[2,512]{1,0:T(2,128)S(1)}, f32[2,512]{1,0:T(2,128)}, u32[]{:S(2)}) copy-start(f32[2,512]{1,0:T(2,128)} %get-tuple-element.42) | copy-start | bytes 12292
  63.8 12.0 %copy-start.18 = (f32[2,512]{1,0:T(2,128)S(1)}, f32[2,512]{1,0:T(2,128)}, u32[]{:S(2)}) copy-start(f32[2,512]{1,0:T(2,128)} %get-tuple-element.43) | copy-start | bytes 12292
  63.8 12.0 %copy-start.19 = (f32[2,512]{1,0:T(2,128)S(1)}, f32[2,512]{1,0:T(2,128)}, u32[]{:S(2)}) copy-start(f32[2,512]{1,0:T(2,128)} %get-tuple-element.44) | copy-start | bytes 12292
  63.8 12.0 %copy-start.20 = (f32[2,512]{1,0:T(2,128)S(1)}, f32[2,512]{1,0:T(2,128)}, u32[]{:S(2)}) copy-start(f32[2,512]{1,0:T(2,128)} %get-tuple-element.45) | copy-start | bytes 12292
  63.8 12.0 %copy-start.21 = (f32[2,512]{1,0:T(2,128)S(1)}, f32[2,512]{1,0:T(2,128)}, u32[]{:S(2)}) copy-start(f32[2,512]{1,0:T(2,128)} %get-tuple-element.46) | copy-start | bytes 12292
  63.8 12.0 %copy-start.22 = (f32[2,512]{1,0:T(2,128)S(1)}, f32[2,512]{1,0:T(2,128)}, u32[]{:S(2)}) copy-start(f32[2,512]{1,0:T(2,128)} %get-tuple-element.47) | copy-start | bytes 12292
  73.8 12.3 %collective-permute-start.1 = (bf16[6,2,128,128]{3,2,0,1:T(8,128)(2,1)S(1)}, bf16[6,2,128,128]{3,2,0,1:T(8,128)(2,1)S(1)}, u32[]{:S(2)}, u32[]{:S(2)}) collective-permute-start(bf16[6,2,128,128]{3,2,0,1:T(8,128)(2,1)S(1)} %fusion.32), channel_id=1, source_target_pairs={{0,16},{8,24},{16,0},{24,8},{32,48},{40,56},{48,32},{56,40},{64,80... | collective-permute-start | bytes 1179656 | tf_op jit(solution)/shard_map/ppermute | solution.py:26
  79.3 82.0 %copy-start.1 = (bf16[2,512,512]{2,1,0:T(8,128)(2,1)}, bf16[2,512,512]{2,1,0:T(8,128)(2,1)S(1)}, u32[]{:S(2)}) copy-start(bf16[2,512,512]{2,1,0:T(8,128)(2,1)S(1)} %multiply_convert_fusion) | copy-start | bytes 3145732
  79.3 8.8 %copy-start.6 = (bf16[512,2,128]{0,2,1:T(8,128)(2,1)S(1)}, bf16[512,2,128]{0,2,1:T(8,128)(2,1)}, u32[]{:S(2)}) copy-start(bf16[512,2,128]{0,2,1:T(8,128)(2,1)} %copy.69) | copy-start | bytes 786436
  86.2 8.5 %collective-permute-start.2 = (bf16[5,2,128,128]{3,2,0,1:T(8,128)(2,1)S(1)}, bf16[5,2,128,128]{3,2,0,1:T(8,128)(2,1)S(1)}, u32[]{:S(2)}, u32[]{:S(2)}) collective-permute-start(bf16[5,2,128,128]{3,2,0,1:T(8,128)(2,1)S(1)} %fusion.34), channel_id=1, source_target_pairs={{0,32},{8,40},{16,48},{24,56},{32,0},{40,8},{48,16},{56,24},{64,96... | collective-permute-start | bytes 983048 | tf_op jit(solution)/shard_map/ppermute | solution.py:26
  94.9 15.7 %collective-permute-start.3 = (bf16[4,2,128,128]{3,2,0,1:T(8,128)(2,1)S(1)}, bf16[4,2,128,128]{3,2,0,1:T(8,128)(2,1)S(1)}, u32[]{:S(2)}, u32[]{:S(2)}) collective-permute-start(bf16[4,2,128,128]{3,2,0,1:T(8,128)(2,1)S(1)} %fusion.36), channel_id=1, source_target_pairs={{0,64},{8,72},{16,80},{24,88},{32,96},{40,104},{48,112},{56,120},{... | collective-permute-start | bytes 786440 | tf_op jit(solution)/shard_map/ppermute | solution.py:26
  110.8 22.7 %collective-permute-start.4 = (bf16[3,2,128,128]{3,2,0,1:T(8,128)(2,1)S(1)}, bf16[3,2,128,128]{3,2,0,1:T(8,128)(2,1)S(1)}, u32[]{:S(2)}, u32[]{:S(2)}) collective-permute-start(bf16[3,2,128,128]{3,2,0,1:T(8,128)(2,1)S(1)} %fusion.37), channel_id=1, source_target_pairs={{0,128},{8,136},{16,144},{24,152},{32,160},{40,168},{48,176},{56,1... | collective-permute-start | bytes 589832 | tf_op jit(solution)/shard_map/ppermute | solution.py:26
  133.5 25.0 %copy-start.5 = (bf16[512,2,128]{2,1,0:T(2,128)(2,1)S(1)}, bf16[512,2,128]{2,1,0:T(2,128)(2,1)}, u32[]{:S(2)}) copy-start(bf16[512,2,128]{2,1,0:T(2,128)(2,1)} %copy-done.4) | copy-start | bytes 786436
  133.5 25.0 %copy-start.16 = (f32[512,2,6]{0,2,1:T(8,128)S(1)}, f32[512,2,6]{0,2,1:T(8,128)}, u32[]{:S(2)}) copy-start(f32[512,2,6]{0,2,1:T(8,128)} %slice.159) | copy-start | bytes 73732
  133.6 23.6 %collective-permute-start.5 = (bf16[2,2,128,128]{3,2,0,1:T(8,128)(2,1)S(1)}, bf16[2,2,128,128]{3,2,0,1:T(8,128)(2,1)S(1)}, u32[]{:S(2)}, u32[]{:S(2)}) collective-permute-start(bf16[2,2,128,128]{3,2,0,1:T(8,128)(2,1)S(1)} %pad_maximum_fusion.5), channel_id=1, source_target_pairs={{0,256},{8,264},{16,272},{24,280},{32,288},{40,296},{48,304},{56,3... | collective-permute-start | bytes 393224 | tf_op jit(solution)/shard_map/ppermute | solution.py:26
where the time goes:
time: 171 us
  waiting for transfers between devices  77.1 us (45%)
  starting transfers between devices  34.9 us (20%)
  matrix products  23.9 us (14%)
  local copies, waits for them, and re-layouts  23 us (13%)
  other arithmetic  10.4 us (6%)
    ppermute x6, waiting for transfers between devices, partner_2(): lax.ppermute(value, axis, [(i, i ^ 1 << bit) for i in range(lax.axis_size...  62.5 us
    ppermute x6, starting transfers between devices, partner_2(): lax.ppermute(value, axis, [(i, i ^ 1 << bit) for i in range(lax.axis_size...  23.7 us
    all_to_all x1, waiting for transfers between devices, sent_to_all(): lax.all_to_all(jnp.broadcast_to(value[None], (peers, *value.shape)), axis...  14.6 us
    all_to_all x1, starting transfers between devices, sent_to_all(): lax.all_to_all(jnp.broadcast_to(value[None], (peers, *value.shape)), axis...  11.2 us
    and x5, other arithmetic, on_device(): chosen = (local_level == level_ix) & causal  8.28 us
    unnamed x51, local copies, waits for them, and re-layouts  4.78 us
    reshape x1, local copies, waits for them, and re-layouts, joined_along(): tiles.reshape(*shape[:dim], shape[dim] * shape[dim + 1], *shape[dim + 2:])  4.21 us
    dot_general x1, matrix products, on_device(): jnp.einsum('thd,shd->hts', cotangent, value_rows, preferred_element_type=...  4.13 us
  transfers between devices with their start and end apart: 7, of which 7 were waited for; matrix products, arithmetic and copies ran while one was open for 12% of the time, Pallas kernels for 0%

commit v1 on v0

v1 whole, which is shorter than its diff:
```python
import functools

import jax
import jax.numpy as jnp
from jax import lax
from jax.experimental import pallas as pl
from jax.experimental.pallas import tpu as pltpu
from jax.sharding import Mesh, PartitionSpec as P

T = 512
D = 128
H = 2
NX = 4
NZ = 16
NY = 4
Q = D // NX
DIRECT = 5 * H * Q
MSG = DIRECT + H * D
F32 = jnp.float32
BF16 = jnp.bfloat16


def dot(a, b):
    return jnp.dot(a, b, preferred_element_type=F32)


def dot_nt(a, b):
    return lax.dot_general(a, b, (((1,), (1,)), ((), ())), preferred_element_type=F32)


def flipped(a):
    return a.astype(F32).T


def level_scale(level):
    return 2.0 ** (-(max(level, 1) - 1) / 2) * D**-0.5


def project_kernel(pos, xa, xb, w, lw, g, q_out, k_out, v_out, msg, x_all):
    core, x = pos[0], pos[1]
    for y in range(NY):
        at_a = pl.multiple_of((2 * y + core) * 256, 256)
        at_b = pl.multiple_of((2 * y + 1 - core) * 256, 256)
        x_all[:, pl.ds(at_a, 256)] = xa[y]
        x_all[:, pl.ds(at_b, 256)] = xb[y]
    q = dot(x_all[...], w[0]).astype(BF16)
    k = dot(x_all[...], w[1]).astype(BF16)
    v = dot(x_all[...], w[2]).astype(BF16)
    q_out[...] = q
    k_out[...] = k
    v_out[...] = v
    for h in range(H):
        cols = slice(h * D, (h + 1) * D)
        q_t = flipped(q[:, cols])
        g_h = g[:, cols]
        mats = [dot(flipped(k[:, cols]).astype(BF16), v[:, cols])]
        for j in range(6):
            row = lw[h, 10 + j : 11 + j, :] * level_scale(10 + j)
            mats.append(dot((q_t * row).astype(BF16), g_h))
        state, r0, r1 = mats[0], mats[1], mats[2]
        for to in range(NX):
            direct = jnp.where(to > x, state, jnp.where((x ^ to) >= 2, r1, r0))
            at = DIRECT + h * D
            msg[to, at : at + D, :] = direct.astype(BF16)
            for m, mat in enumerate([state] + mats[3:]):
                at = (m * H + h) * Q
                msg[to, at : at + Q, :] = mat[to * Q : (to + 1) * Q].astype(BF16)


def spread_kernel(pos, recv, out, mats):
    z = pos[2]
    total = recv[0, :DIRECT, :].astype(F32)
    for src in range(1, NX):
        total = total + recv[src, :DIRECT, :].astype(F32)
    mats[...] = total.astype(BF16).reshape(5, H * Q, D)
    for to in range(NZ):
        d = z ^ to
        top = (d >= 2).astype(jnp.int32) + (d >= 4).astype(jnp.int32) + (d >= 8).astype(jnp.int32)
        out[to] = mats[jnp.where(to > z, 0, 1 + top)]


def collect_kernel(pos, recv, out):
    z = pos[2]
    for j in range(4):
        first = lax.shift_left(lax.shift_right_logical(z, j) ^ 1, j)
        total = recv[first].astype(F32)
        for i in range(1, 2**j):
            total = total + recv[first + i].astype(F32)
        total = total.astype(BF16)
        for to in range(NX):
            out[to, j * H * Q : (j + 1) * H * Q, :] = total


def attend_kernel(q_in, k_in, v_in, g_in, lw, out_t, dq_t, dk, dv, a_t, b_t):
    n = T // D
    s_at = lax.broadcasted_iota(jnp.int32, (D, D), 0)
    t_at = lax.broadcasted_iota(jnp.int32, (D, D), 1)
    differ = s_at ^ t_at
    for h in range(H):
        cols = slice(h * D, (h + 1) * D)
        q, k, v, g = q_in[:, cols], k_in[:, cols], v_in[:, cols], g_in[:, cols]
        q_t, k_t, v_t, g_t = (flipped(a).astype(BF16) for a in (q, k, v, g))
        rows = [lw[h, l : l + 1, :] * level_scale(l) for l in range(10)]
        for si in range(n):
            s = slice(si * D, (si + 1) * D)
            scores = dot(k[s], q_t[:, si * D :])
            back = dot(v[s], g_t[:, si * D :])
            for ti in range(si, n):
                t = slice(ti * D, (ti + 1) * D)
                part = slice((ti - si) * D, (ti - si + 1) * D)
                if ti == si:
                    mask = jnp.broadcast_to(rows[0][:, t], (D, D))
                    for l in range(1, 8):
                        mask = jnp.where(differ >= 2 ** (l - 1), rows[l][:, t], mask)
                    mask = jnp.where(t_at >= s_at, mask, 0.0)
                else:
                    mask = rows[8 if ti ^ si == 1 else 9][:, t]
                a_t[s, t] = (scores[:, part] * mask).astype(BF16)
                b_t[s, t] = (back[:, part] * mask).astype(BF16)
            dv[s, cols] = dot(a_t[s, si * D :], g[si * D :])
            dk[s, cols] = dot(b_t[s, si * D :], q[si * D :])
        for ti in range(n):
            t = slice(ti * D, (ti + 1) * D)
            seen = (ti + 1) * D
            out_t[h, :, t] = dot(v_t[:, :seen], a_t[:seen, t])
            dq_t[h, :, t] = dot(k_t[:, :seen], b_t[:seen, t])


def finish_kernel(pos, q_in, k_in, v_in, g_in, lw, recv_a, recv_c, out_p, dq_p, dk_p, dv_p, out, dq, dk, dv):
    x, n = pos[1], pos[3]
    for h in range(H):
        cols = slice(h * D, (h + 1) * D)
        at = DIRECT + h * D
        near = [recv_a[x ^ i, at : at + D, :].astype(F32) for i in (1, 2, 3)]
        slots = [near[0], near[1] + near[2]]
        for j in range(4):
            at = (j * H + h) * Q
            slots.append(
                jnp.concatenate([recv_c[src, at : at + Q, :].astype(F32) for src in range(NX)], 0)
            )
        q_t, g_t = flipped(q_in[:, cols]), flipped(g_in[:, cols])
        total_o, total_q = out_p[h], dq_p[h]
        later = jnp.zeros((D, D), F32)
        for j in range(6):
            flag = (lax.shift_right_logical(n, j) & 1).astype(F32)
            row = lw[h, 10 + j : 11 + j, :] * (level_scale(10 + j) * flag)
            total_o = total_o + dot(slots[j].T.astype(BF16), (q_t * row).astype(BF16))
            total_q = total_q + dot(slots[j].astype(BF16), (g_t * row).astype(BF16))
            later = later + slots[j] * (1.0 - flag)
        later = later.astype(BF16)
        out[:, cols] = total_o.T.astype(BF16)
        dq[:, cols] = total_q.T.astype(BF16)
        dk[:, cols] = (dk_p[:, cols] + dot_nt(v_in[:, cols], later)).astype(BF16)
        dv[:, cols] = (dv_p[:, cols] + dot(k_in[:, cols], later)).astype(BF16)


SMEM = pl.BlockSpec(memory_space=pltpu.SMEM)
VMEM = pl.BlockSpec(memory_space=pltpu.VMEM)


def call(kernel, pos, args, outs, scratch=()):
    shapes = tuple(jax.ShapeDtypeStruct(s, d) for s, d in outs)
    head = () if pos is None else (pos,)
    return pl.pallas_call(
        kernel,
        out_shape=shapes,
        in_specs=[SMEM] * len(head) + [VMEM] * len(args),
        out_specs=tuple(VMEM for _ in shapes),
        scratch_shapes=list(scratch),
        compiler_params=pltpu.CompilerParams(vmem_limit_bytes=40 * 2**20),
    )(*head, *args)


def swap(value, axis):
    return lax.all_to_all(value, axis, 0, 0, tiled=True)


def on_device(activations, w_proj, level_weight, g):
    z, x, core = lax.axis_index("z"), lax.axis_index("x"), lax.axis_index("core")
    pos = jnp.stack([core, x, z, z * NX + x]).astype(jnp.int32)
    lw = jnp.transpose(level_weight, (1, 2, 0))
    xa = swap(jnp.broadcast_to(activations[None], (NY, *activations.shape)), "y")
    xb = lax.ppermute(xa, "core", [(0, 1), (1, 0)])
    tokens = ((T, H * D), BF16)
    q, k, v, msg = call(
        project_kernel,
        pos,
        (xa, xb, w_proj, lw, g),
        (tokens, tokens, tokens, ((NX, MSG, D), BF16)),
        [pltpu.VMEM((T, 2048), BF16)],
    )
    recv_a = swap(msg, "x")
    (far,) = call(
        spread_kernel, pos, (recv_a,), (((NZ, H * Q, D), BF16),), [pltpu.VMEM((5, H * Q, D), BF16)]
    )
    recv_b = swap(far, "z")
    (back,) = call(collect_kernel, pos, (recv_b,), (((NX, 4 * H * Q, D), BF16),))
    recv_c = swap(back, "x")
    flat, tall = ((T, H * D), F32), ((H, D, T), F32)
    parts = call(
        attend_kernel,
        None,
        (q, k, v, g, lw),
        (tall, tall, flat, flat),
        [pltpu.VMEM((T, T), BF16), pltpu.VMEM((T, T), BF16)],
    )
    return call(
        finish_kernel, pos, (q, k, v, g, lw, recv_a, recv_c, *parts), (tokens,) * 4
    )


def solution(mesh):
    fine = Mesh(mesh.devices.reshape(NZ, NX, NY, 2), ("z", "x", "y", "core"))
    rows, cols = ("z", "x"), ("y", "core")
    in_specs = (P(rows, cols), P(None, None, cols), P(rows, cols, None), P(rows, cols))
    return jax.shard_map(
        on_device, mesh=fine, in_specs=in_specs, out_specs=(P(rows, cols),) * 4, check_vma=False
    )
```

time: 171 us -> 96 us (0.56)
  the two profiles are of different devices: /device:TPU:1 before, /device:TPU:32 now
where the time goes in v1:
time: 96 us; the launch traced here: 95.5 us
  blocking collectives  66.4 us (69%)
  Pallas kernels  10.9 us (11%)
  local copies, waits for them, and re-layouts  6.61 us (7%)
  waiting for transfers between devices  5.45 us (6%)
  starting transfers between devices  5.32 us (6%)
    all_to_all x3, blocking collectives, swap(): return lax.all_to_all(value, axis, 0, 0, tiled=True)  66.4 us
    pallas_call x5, Pallas kernels, call(): pl.pallas_call(kernel, out_shape=shapes, in_specs=[SMEM] * len(head) + [V...  10.9 us
    unnamed x14, local copies, waits for them, and re-layouts  5.54 us
    all_to_all x1, starting transfers between devices, swap(): return lax.all_to_all(value, axis, 0, 0, tiled=True)  3.41 us
    all_to_all x1, waiting for transfers between devices, swap(): return lax.all_to_all(value, axis, 0, 0, tiled=True)  2.91 us
    ppermute x1, waiting for transfers between devices, on_device(): xb = lax.ppermute(xa, 'core', [(0, 1), (1, 0)])  2.54 us
  transfers between devices with their start and end apart: 2, of which 2 were waited for; matrix products, arithmetic and copies ran while one was open for 0% of the time, Pallas kernels for 2%

profile of v1, /device:TPU:32, one launch (start us, length us, event | category | flops | bytes accessed | tf_op | source)
XLA Modules:
  0.0 95.5 jit_solution(8017041464769163906)
XLA Ops:
  0.6 0.0 copy-start.1
  0.6 0.0 copy-start.2
  0.7 1.1 %broadcast_in_dim.2 = bf16[4,512,256]{2,1,0:T(8,128)(2,1)S(1)} broadcast(bf16[512,256]{1,0:T(8,128)(2,1)} %param.4), dimensions={1,2} | broadcast | bytes 1310720 | tf_op jit(solution)/shard_map/broadcast_in_dim | solution.py:182
  1.7 19.4 %all_to_all.20.xa = bf16[4,512,256]{2,1,0:T(8,128)(2,1)S(1)} all-to-all(bf16[4,512,256]{2,1,0:T(8,128)(2,1)S(1)} %broadcast_in_dim.2), channel_id=1, replica_groups=mesh['z'=16,'x'=4,'y'=4,'core'=2] {'y'}, dimensions={0} | all-to-all | bytes 2097152 | tf_op jit(solution)/shard_map/all_to_all | solution.py:175
  21.1 1.9 %collective-permute-start = (bf16[4,512,256]{2,1,0:T(8,128)(2,1)S(1)}, bf16[4,512,256]{2,1,0:T(8,128)(2,1)S(1)}, u32[]{:S(2)}, u32[]{:S(2)}) collective-permute-start(bf16[4,512,256]{2,1,0:T(8,128)(2,1)S(1)} %all_to_all.20.xa), channel_id=1, source_target_pairs={{0,1},{1,0},{2,3},{3,2},{4,5},{5,4},{6,7},{7,6},{8,9},{9,8},{10,11... | collective-permute-start | bytes 3145736 | tf_op jit(solution)/shard_map/ppermute | solution.py:183
  23.0 0.1 pad_add_fusion.pos
  23.1 2.5 %collective-permute-done.xb = bf16[4,512,256]{2,1,0:T(8,128)(2,1)S(1)} collective-permute-done((bf16[4,512,256]{2,1,0:T(8,128)(2,1)S(1)}, bf16[4,512,256]{2,1,0:T(8,128)(2,1)S(1)}, u32[]{:S(2)}, u32[]{:S(2)}) %collective-permute-start) | collective-permute-done | bytes 1048608 | tf_op jit(solution)/shard_map/ppermute | solution.py:183
  25.6 0.0 copy-done.1
  25.6 0.0 copy-done.2
  25.6 0.0 copy-start
  25.6 1.9 %copy-done = bf16[3,2048,256]{2,1,0:T(8,128)(2,1)S(1)} copy-done((bf16[3,2048,256]{2,1,0:T(8,128)(2,1)S(1)}, bf16[3,2048,256]{2,1,0:T(8,128)(2,1)}, u32[]{:S(2)}) %copy-start) | copy-done | bytes 3145752
  27.5 4.1 %shard_map.75 = (bf16[512,256]{1,0:T(8,128)(2,1)S(1)}, bf16[512,256]{1,0:T(8,128)(2,1)S(1)}, bf16[512,256]{1,0:T(8,128)(2,1)S(1)}, bf16[4,576,128]{2,1,0:T(8,128)(2,1)S(1)}) custom-call(s32[4]{0:T(128)S(1)} %pad_add_fusion.pos, bf16[4,512,256]{2,1,0:T(8,128)(2,1)S(1)} %all_to_all.20.xa, bf16[4,512,256]{2,1,0:T(8,128)(2,1)S(1)} %collective-permute-done.xb, ...), custom_call_target="tpu_custom_call" | custom-call | tf_op jit(solution)/shard_map/pallas_call | solution.py:164
  31.6 14.6 %all_to_all.21.recv.recv_a = bf16[4,576,128]{2,1,0:T(8,128)(2,1)S(1)} all-to-all(bf16[4,576,128]{2,1,0:T(8,128)(2,1)S(1)} %get-tuple-element.15), channel_id=1, replica_groups=mesh['z'=16,'x'=4,'y'=4,'core'=2] {'x'}, dimensions={0} | all-to-all | bytes 1179648 | tf_op jit(solution)/shard_map/all_to_all | solution.py:175
  46.2 0.6 shard_map.76
  46.9 32.5 %all_to_all.22.recv = bf16[16,64,128]{2,1,0:T(8,128)(2,1)S(1)} all-to-all(bf16[16,64,128]{2,1,0:T(8,128)(2,1)S(1)} %shard_map.76), channel_id=1, replica_groups=mesh['z'=16,'x'=4,'y'=4,'core'=2] {'z'}, dimensions={0} | all-to-all | bytes 524288 | tf_op jit(solution)/shard_map/all_to_all | solution.py:175
  79.4 1.3 %shard_map.77 = bf16[4,256,128]{2,1,0:T(8,128)(2,1)} custom-call(s32[4]{0:T(128)S(1)} %pad_add_fusion.pos, bf16[16,64,128]{2,1,0:T(8,128)(2,1)S(1)} %all_to_all.22.recv), custom_call_target="tpu_custom_call" | custom-call | tf_op jit(solution)/shard_map/pallas_call | solution.py:164
  80.6 3.4 %all-to-all-start.3 = ((bf16[4,256,128]{2,1,0:T(8,128)(2,1)}), bf16[4,256,128]{2,1,0:T(8,128)(2,1)S(1)}, u32[]{:S(2)}, u32[]{:S(2)}) async-start(bf16[4,256,128]{2,1,0:T(8,128)(2,1)} %shard_map.77), calls=%async_computation.3 | async-start | bytes 524288 | tf_op jit(solution)/shard_map/all_to_all | solution.py:175
  84.1 2.2 %shard_map.78 = (f32[2,128,512]{2,1,0:T(8,128)S(1)}, f32[2,128,512]{2,1,0:T(8,128)S(1)}, f32[512,256]{1,0:T(8,128)S(1)}, f32[512,256]{1,0:T(8,128)S(1)}) custom-call(bf16[512,256]{1,0:T(8,128)(2,1)S(1)} %get-tuple-element.12.q_in, bf16[512,256]{1,0:T(8,128)(2,1)S(1)} %get-tuple-element.13.k_in, bf16[512,256]{1,0:T(8,128)(2,1)S(1)} %get-tuple-element.14.v_in, ...), custom_call_target="tpu_custom_call" | custom-call | tf_op jit(solution)/shard_map/pallas_call | solution.py:164
  86.2 0.0 copy-start.3
  86.2 0.8 copy-done.3
  87.0 0.0 copy-start.5
  87.0 0.8 copy-done.5
  87.8 2.9 %all-to-all-done.3.recv_c = bf16[4,256,128]{2,1,0:T(8,128)(2,1)S(1)} async-done(((bf16[4,256,128]{2,1,0:T(8,128)(2,1)}), bf16[4,256,128]{2,1,0:T(8,128)(2,1)S(1)}, u32[]{:S(2)}, u32[]{:S(2)}) %all-to-all-start.3) | async-done | bytes 262176 | tf_op jit(solution)/shard_map/all_to_all | solution.py:175
  90.7 0.0 copy-start.4
  90.7 1.0 %copy-done.4 = f32[512,256]{1,0:T(8,128)S(1)} copy-done((f32[512,256]{1,0:T(8,128)S(1)}, f32[512,256]{1,0:T(8,128)}, u32[]{:S(2)}) %copy-start.4) | copy-done | bytes 524312
  91.7 0.0 copy-start.6
  91.7 1.0 %copy-done.6 = f32[512,256]{1,0:T(8,128)S(1)} copy-done((f32[512,256]{1,0:T(8,128)S(1)}, f32[512,256]{1,0:T(8,128)}, u32[]{:S(2)}) %copy-start.6) | copy-done | bytes 524312
  92.8 2.7 %shard_map.79 = (bf16[512,256]{1,0:T(8,128)(2,1)}, bf16[512,256]{1,0:T(8,128)(2,1)}, bf16[512,256]{1,0:T(8,128)(2,1)}, bf16[512,256]{1,0:T(8,128)(2,1)}) custom-call(s32[4]{0:T(128)S(1)} %pad_add_fusion.pos, bf16[512,256]{1,0:T(8,128)(2,1)S(1)} %get-tuple-element.12.q_in, bf16[512,256]{1,0:T(8,128)(2,1)S(1)} %get-tuple-element.13.k_in, ...), custom_call_target="tpu_custom_call" | custom-call | tf_op jit(solution)/shard_map/pallas_call | solution.py:164
Async XLA Ops:
  0.6 25.0 %copy-start.1 = (bf16[512,256]{1,0:T(8,128)(2,1)S(1)}, bf16[512,256]{1,0:T(8,128)(2,1)}, u32[]{:S(2)}) copy-start(bf16[512,256]{1,0:T(8,128)(2,1)} %g_in.3) | copy-start | bytes 786436
  0.6 25.0 %copy-start.2 = (f32[512,2,16]{0,2,1:T(8,128)S(1)}, f32[512,2,16]{0,2,1:T(8,128)}, u32[]{:S(2)}) copy-start(f32[512,2,16]{0,2,1:T(8,128)} %param.6) | copy-start | bytes 196612
  21.1 4.5 %collective-permute-start = (bf16[4,512,256]{2,1,0:T(8,128)(2,1)S(1)}, bf16[4,512,256]{2,1,0:T(8,128)(2,1)S(1)}, u32[]{:S(2)}, u32[]{:S(2)}) collective-permute-start(bf16[4,512,256]{2,1,0:T(8,128)(2,1)S(1)} %all_to_all.20.xa), channel_id=1, source_target_pairs={{0,1},{1,0},{2,3},{3,2},{4,5},{5,4},{6,7},{7,6},{8,9},{9,8},{10,11... | collective-permute-start | bytes 3145736 | tf_op jit(solution)/shard_map/ppermute | solution.py:183
  25.6 1.9 %copy-start = (bf16[3,2048,256]{2,1,0:T(8,128)(2,1)S(1)}, bf16[3,2048,256]{2,1,0:T(8,128)(2,1)}, u32[]{:S(2)}) copy-start(bf16[3,2048,256]{2,1,0:T(8,128)(2,1)} %w.1) | copy-start | bytes 9437188
  80.6 10.1 %all-to-all-start.3 = ((bf16[4,256,128]{2,1,0:T(8,128)(2,1)}), bf16[4,256,128]{2,1,0:T(8,128)(2,1)S(1)}, u32[]{:S(2)}, u32[]{:S(2)}) async-start(bf16[4,256,128]{2,1,0:T(8,128)(2,1)} %shard_map.77), calls=%async_computation.3 | async-start | bytes 524288 | tf_op jit(solution)/shard_map/all_to_all | solution.py:175
  86.2 0.8 copy-start.3
  87.0 0.8 copy-start.5
  90.7 1.0 %copy-start.4 = (f32[512,256]{1,0:T(8,128)S(1)}, f32[512,256]{1,0:T(8,128)}, u32[]{:S(2)}) copy-start(f32[512,256]{1,0:T(8,128)} %copy-done.3) | copy-start | bytes 1572868
  91.7 1.0 %copy-start.6 = (f32[512,256]{1,0:T(8,128)S(1)}, f32[512,256]{1,0:T(8,128)}, u32[]{:S(2)}) copy-start(f32[512,256]{1,0:T(8,128)} %copy-done.5) | copy-start | bytes 1572868

commit v2 on v1

v2 whole, which is shorter than its diff:
```python
import jax
import jax.numpy as jnp
from jax import lax
from jax.experimental import pallas as pl
from jax.experimental.pallas import tpu as pltpu
from jax.sharding import Mesh, PartitionSpec as P

T = 512
D = 128
H = 2
NX = 4
NL = 2
NG = NX * NL
NZ = 8
NY = 4
Q = D // NG
HQ = H * Q
F32 = jnp.float32
BF16 = jnp.bfloat16


def dot(a, b):
    return jnp.dot(a, b, preferred_element_type=F32)


def dot_nt(a, b):
    return lax.dot_general(a, b, (((1,), (1,)), ((), ())), preferred_element_type=F32)


def flipped(a):
    return a.astype(F32).T


def level_scale(level):
    return 2.0 ** (-(max(level, 1) - 1) / 2) * D**-0.5


def half_kernel(pos, xa, w, lw, g, part, w_rest, g6, w_mine, sems):
    core = pos[0]
    copies = [
        pltpu.make_async_copy(w.at[c, :, side], to.at[c], sems.at[i, c])
        for i, (side, to) in enumerate(((core, w_mine), (1 - core, w_rest)))
        for c in range(3)
    ]
    for copy in copies:
        copy.start()
    for h in range(H):
        g_t = flipped(g[:, h * D : (h + 1) * D])
        for j in range(6):
            row = lw[h, 10 + j : 11 + j, :] * level_scale(10 + j)
            g6[h, j * D : (j + 1) * D, :] = (g_t * row).astype(BF16)
    rows = jnp.concatenate([xa[y] for y in range(NY)], 1)
    for c in range(3):
        copies[c].wait()
        part[c] = dot(rows, w_mine[c].reshape(NY * 256, 256))
    for copy in copies[3:]:
        copy.wait()


def project_kernel(xb, w_rest, part, g6, qkv, msg):
    rows = jnp.concatenate([xb[y] for y in range(NY)], 1)
    for c in range(3):
        total = part[c] + dot(rows, w_rest[c].reshape(NY * 256, 256))
        qkv[c] = total.astype(BF16)
    for h in range(H):
        cols = slice(h * D, (h + 1) * D)
        k_t = flipped(qkv[1, :, cols]).astype(BF16)
        state = dot(k_t, qkv[2, :, cols]).astype(BF16)
        grads = dot(g6[h], qkv[0, :, cols]).astype(BF16)
        mats = [state] + [grads[j * D : (j + 1) * D] for j in range(6)]
        for m, mat in enumerate(mats):
            at = m * HQ + h * Q
            for to in range(NG):
                msg[to, at : at + Q, :] = mat[to * Q : (to + 1) * Q]


def spread_kernel(pos, recv, far, low, mats):
    z = pos[1]

    def total(m, sources):
        terms = [recv[s, m * HQ : (m + 1) * HQ, :].astype(F32) for s in sources]
        return sum(terms[1:], terms[0])

    mats[0] = total(0, range(NG)).astype(BF16)
    for m in range(3):
        mats[1 + m] = total(4 + m, range(NG)).astype(BF16)
    for to in range(NZ):
        d = z ^ to
        top = (d >= 2).astype(jnp.int32) + (d >= 4).astype(jnp.int32)
        far[to] = mats[jnp.where(to > z, 0, 1 + top)]
    for j in range(3):
        for first in range(0, NG, 2**j):
            sent = total(1 + j if (first >> j) & 1 else 0, range(first, first + 2**j))
            for to in range(first ^ 2**j, (first ^ 2**j) + 2**j):
                low[to, j * HQ : (j + 1) * HQ, :] = sent.astype(BF16)


def collect_kernel(pos, recv, low, out):
    z = pos[1]
    out[:, : 3 * HQ, :] = low[...]
    for j in range(3):
        first = lax.shift_left(lax.shift_right_logical(z, j) ^ 1, j)
        total = recv[first].astype(F32)
        for i in range(1, 2**j):
            total = total + recv[first + i].astype(F32)
        total = total.astype(BF16)
        for to in range(NG):
            out[to, (j + 3) * HQ : (j + 4) * HQ, :] = total


def attend_kernel(qkv, g_in, lw, out_t, dq_t, dk, dv, a_t, b_t):
    n = T // D
    s_at = lax.broadcasted_iota(jnp.int32, (D, D), 0)
    t_at = lax.broadcasted_iota(jnp.int32, (D, D), 1)
    differ = s_at ^ t_at
    for h in range(H):
        cols = slice(h * D, (h + 1) * D)
        q, k, v, g = qkv[0, :, cols], qkv[1, :, cols], qkv[2, :, cols], g_in[:, cols]
        q_t, k_t, v_t, g_t = (flipped(a).astype(BF16) for a in (q, k, v, g))
        rows = [lw[h, l : l + 1, :] * level_scale(l) for l in range(10)]
        for si in range(n):
            s = slice(si * D, (si + 1) * D)
            scores = dot(k[s], q_t[:, si * D :])
            back = dot(v[s], g_t[:, si * D :])
            for ti in range(si, n):
                t = slice(ti * D, (ti + 1) * D)
                part = slice((ti - si) * D, (ti - si + 1) * D)
                if ti == si:
                    mask = jnp.broadcast_to(rows[0][:, t], (D, D))
                    for l in range(1, 8):
                        mask = jnp.where(differ >= 2 ** (l - 1), rows[l][:, t], mask)
                    mask = jnp.where(t_at >= s_at, mask, 0.0)
                else:
                    mask = rows[8 if ti ^ si == 1 else 9][:, t]
                a_t[s, t] = (scores[:, part] * mask).astype(BF16)
                b_t[s, t] = (back[:, part] * mask).astype(BF16)
            dv[s, cols] = dot(a_t[s, si * D :], g[si * D :]).astype(BF16)
            dk[s, cols] = dot(b_t[s, si * D :], q[si * D :]).astype(BF16)
        for ti in range(n):
            t = slice(ti * D, (ti + 1) * D)
            seen = (ti + 1) * D
            out_t[h, :, t] = dot(v_t[:, :seen], a_t[:seen, t]).astype(BF16)
            dq_t[h, :, t] = dot(k_t[:, :seen], b_t[:seen, t]).astype(BF16)


def finish_kernel(pos, qkv, g_in, lw, recv_c, out_p, dq_p, dk_p, dv_p, out, dq, dk, dv):
    n = pos[2]
    for h in range(H):
        cols = slice(h * D, (h + 1) * D)
        slots = []
        for j in range(6):
            at = j * HQ + h * Q
            slots.append(
                jnp.concatenate([recv_c[src, at : at + Q, :].astype(F32) for src in range(NG)], 0)
            )
        q_t, g_t = flipped(qkv[0, :, cols]), flipped(g_in[:, cols])
        later = jnp.zeros((D, D), F32)
        reads_o, reads_q = [], []
        for j in range(6):
            flag = (lax.shift_right_logical(n, j) & 1).astype(F32)
            row = lw[h, 10 + j : 11 + j, :] * (level_scale(10 + j) * flag)
            reads_o.append((q_t * row).astype(BF16))
            reads_q.append((g_t * row).astype(BF16))
            later = later + slots[j] * (1.0 - flag)
        states = jnp.concatenate(slots, 1).astype(BF16)
        states_t = jnp.concatenate([s.T for s in slots], 1).astype(BF16)
        total_o = out_p[h].astype(F32) + dot(states_t, jnp.concatenate(reads_o, 0))
        total_q = dq_p[h].astype(F32) + dot(states, jnp.concatenate(reads_q, 0))
        later = later.astype(BF16)
        out[:, cols] = total_o.T.astype(BF16)
        dq[:, cols] = total_q.T.astype(BF16)
        dk[:, cols] = (dk_p[:, cols] + dot(qkv[2, :, cols], later)).astype(BF16)
        dv[:, cols] = (dv_p[:, cols] + dot_nt(qkv[1, :, cols], later)).astype(BF16)


SMEM = pl.BlockSpec(memory_space=pltpu.SMEM)
VMEM = pl.BlockSpec(memory_space=pltpu.VMEM)
LEFT = pl.BlockSpec(memory_space=pltpu.HBM)


def call(kernel, pos, args, outs, scratch=(), mib=8, flops=0, left=()):
    shapes = tuple(jax.ShapeDtypeStruct(s, d) for s, d in outs)
    head = () if pos is None else (pos,)
    moved = sum(a.size * a.dtype.itemsize for a in (*args, *shapes))
    return pl.pallas_call(
        kernel,
        out_shape=shapes,
        in_specs=[SMEM] * len(head) + [LEFT if i in left else VMEM for i in range(len(args))],
        out_specs=tuple(VMEM for _ in shapes),
        scratch_shapes=list(scratch),
        cost_estimate=pl.CostEstimate(flops=flops, bytes_accessed=moved, transcendentals=0),
        compiler_params=pltpu.CompilerParams(vmem_limit_bytes=mib * 2**20),
    )(*head, *args)


def swap(value, axis):
    return lax.all_to_all(value, axis, 0, 0, tiled=True)


def body(activations, w_proj, level_weight, g):
    zh, zl, x, core = (lax.axis_index(a) for a in ("zh", "zl", "x", "core"))
    pos = jnp.stack([core, zh, (zh * NL + zl) * NX + x]).astype(jnp.int32)
    lw = jnp.transpose(level_weight, (1, 2, 0))
    w = w_proj.reshape(3, NY, 2, 256, 256)
    half_flops = T * 1024 * 768 * 2
    xa = swap(jnp.broadcast_to(activations[None], (NY, *activations.shape)), "y")
    xb = lax.ppermute(xa, "core", [(0, 1), (1, 0)])
    part, w_rest, g6 = call(
        half_kernel,
        pos,
        (xa, w, lw, g),
        (((3, T, H * D), F32), ((3, NY, 256, 256), BF16), ((H, 6 * D, T), BF16)),
        [pltpu.VMEM((3, NY, 256, 256), BF16), pltpu.SemaphoreType.DMA((2, 3))],
        mib=47,
        flops=half_flops,
        left=(1,),
    )
    qkv, msg = call(
        project_kernel,
        None,
        (xb, w_rest, part, g6),
        (((3, T, H * D), BF16), ((NG, 7 * HQ, D), BF16)),
        flops=half_flops,
    )
    recv_a = swap(msg, ("zl", "x"))
    far, low = call(
        spread_kernel,
        pos,
        (recv_a,),
        (((NZ, HQ, D), BF16), ((NG, 3 * HQ, D), BF16)),
        [pltpu.VMEM((4, HQ, D), BF16)],
    )
    recv_b = swap(far, "zh")
    (back,) = call(collect_kernel, pos, (recv_b, low), (((NG, 6 * HQ, D), BF16),))
    recv_c = swap(back, ("zl", "x"))
    flat, tall = ((T, H * D), BF16), ((H, D, T), BF16)
    parts = call(
        attend_kernel,
        None,
        (qkv, g, lw),
        (tall, tall, flat, flat),
        [pltpu.VMEM((T, T), BF16), pltpu.VMEM((T, T), BF16)],
        flops=2 * H * 6 * T * T * D,
    )
    return call(finish_kernel, pos, (qkv, g, lw, recv_c, *parts), (((T, H * D), BF16),) * 4)


def solution(mesh):
    fine = Mesh(mesh.devices.reshape(NZ, NL, NX, NY, 2), ("zh", "zl", "x", "y", "core"))
    rows, cols = ("zh", "zl", "x"), ("y", "core")
    in_specs = (P(rows, cols), P(None, None, cols), P(rows, cols, None), P(rows, cols))
    return jax.shard_map(
        body, mesh=fine, in_specs=in_specs, out_specs=(P(rows, cols),) * 4, check_vma=False
    )
```

time: 96 us -> 86.4 us (0.900)
  the two profiles are of different devices: /device:TPU:32 before, /device:TPU:8 now
where the time goes in v2:
time: 86.4 us; the launch traced here: 86 us
  blocking collectives  61.2 us (71%)
  Pallas kernels  12.1 us (14%)
  waiting for transfers between devices  5.51 us (6%)
  starting transfers between devices  5.36 us (6%)
  local copies, waits for them, and re-layouts  1.07 us (1%)
    all_to_all x3, blocking collectives, swap(): return lax.all_to_all(value, axis, 0, 0, tiled=True)  61.2 us
    pallas_call x6, Pallas kernels, call(): pl.pallas_call(kernel, out_shape=shapes, in_specs=[SMEM] * len(head) + [L...  12.1 us
    all_to_all x1, waiting for transfers between devices, swap(): return lax.all_to_all(value, axis, 0, 0, tiled=True)  5.5 us
    all_to_all x1, starting transfers between devices, swap(): return lax.all_to_all(value, axis, 0, 0, tiled=True)  3.45 us
    ppermute x1, starting transfers between devices, body(): xb = lax.ppermute(xa, 'core', [(0, 1), (1, 0)])  1.91 us
  transfers between devices with their start and end apart: 2, of which 1 were waited for; matrix products, arithmetic and copies ran while one was open for 0% of the time, Pallas kernels for 7%

profile of v2, /device:TPU:8, one launch (start us, length us, event | category | flops | bytes accessed | tf_op | source)
XLA Modules:
  0.0 86.0 jit_solution(6099528759682781626)
XLA Ops:
  0.6 0.0 copy-start
  0.6 0.0 copy-start.1
  0.7 1.1 %broadcast_in_dim.2 = bf16[4,512,256]{2,1,0:T(8,128)(2,1)S(1)} broadcast(bf16[512,256]{1,0:T(8,128)(2,1)} %param.4), dimensions={1,2} | broadcast | bytes 1310720 | tf_op jit(solution)/shard_map/broadcast_in_dim | solution.py:206
  1.7 18.3 %all_to_all.20.xa = bf16[4,512,256]{2,1,0:T(8,128)(2,1)S(1)} all-to-all(bf16[4,512,256]{2,1,0:T(8,128)(2,1)S(1)} %broadcast_in_dim.2), channel_id=1, replica_groups=mesh['zh'=8,'zl'=2,'x'=4,'y'=4,'core'=2] {'y'}, dimensions={0} | all-to-all | bytes 2097152 | tf_op jit(solution)/shard_map/all_to_all | solution.py:197
  20.1 1.9 %collective-permute-start = (bf16[4,512,256]{2,1,0:T(8,128)(2,1)S(1)}, bf16[4,512,256]{2,1,0:T(8,128)(2,1)S(1)}, u32[]{:S(2)}, u32[]{:S(2)}) collective-permute-start(bf16[4,512,256]{2,1,0:T(8,128)(2,1)S(1)} %all_to_all.20.xa), channel_id=1, source_target_pairs={{0,1},{1,0},{2,3},{3,2},{4,5},{5,4},{6,7},{7,6},{8,9},{9,8},{10,11... | collective-permute-start | bytes 3145736 | tf_op jit(solution)/shard_map/ppermute | solution.py:207
  22.0 0.1 pad_add_fusion.pos
  22.1 0.0 copy-done
  22.1 0.0 copy-done.1
  22.1 3.5 %shard_map.75 = (f32[3,512,256]{2,1,0:T(8,128)S(1)}, bf16[3,4,256,256]{3,2,1,0:T(8,128)(2,1)S(1)}, bf16[2,768,512]{2,1,0:T(8,128)(2,1)S(1)}) custom-call(s32[3]{0:T(128)S(1)} %pad_add_fusion.pos, bf16[4,512,256]{2,1,0:T(8,128)(2,1)S(1)} %all_to_all.20.xa, bf16[3,4,2,256,256]{4,3,2,1,0:T(8,128)(2,1)} %bitcast.8, f32[2,16,512]{2,1,0:T(8,128)S(1)} %bitcast.5, ...), custom_call_target="tpu_custom_call" | custom-call | flops 805306368 | bytes 9240576 | tf_op jit(solution)/shard_map/pallas_call | solution.py:185
  25.5 0.0 collective-permute-done.xb
  25.6 2.2 %shard_map.76 = (bf16[3,512,256]{2,1,0:T(8,128)(2,1)S(1)}, bf16[8,224,128]{2,1,0:T(8,128)(2,1)S(1)}) custom-call(bf16[4,512,256]{2,1,0:T(8,128)(2,1)S(1)} %collective-permute-done.xb, bf16[3,4,256,256]{3,2,1,0:T(8,128)(2,1)S(1)} %get-tuple-element.15.w_rest, f32[3,512,256]{2,1,0:T(8,128)S(1)} %get-tuple-element.16.part, ...), custom_call_target="tpu_custom_call" | custom-call | flops 805306368 | bytes 7012352 | tf_op jit(solution)/shard_map/pallas_call | solution.py:185
  27.7 15.5 %all_to_all.21.recv = bf16[8,224,128]{2,1,0:T(8,128)(2,1)S(1)} all-to-all(bf16[8,224,128]{2,1,0:T(8,128)(2,1)S(1)} %get-tuple-element.19), channel_id=1, replica_groups=mesh['zh'=8,'zl'=2,'x'=4,'y'=4,'core'=2] {'zl','x'}, dimensions={0} | all-to-all | bytes 917504 | tf_op jit(solution)/shard_map/all_to_all | solution.py:197
  43.2 0.6 shard_map.77
  43.8 27.3 %all_to_all.22.recv = bf16[8,32,128]{2,1,0:T(8,128)(2,1)S(1)} all-to-all(bf16[8,32,128]{2,1,0:T(8,128)(2,1)S(1)} %get-tuple-element.20), channel_id=1, replica_groups=mesh['zh'=8,'zl'=2,'x'=4,'y'=4,'core'=2] {'zh'}, dimensions={0} | all-to-all | bytes 131072 | tf_op jit(solution)/shard_map/all_to_all | solution.py:197
  71.2 1.3 %shard_map.78 = bf16[8,192,128]{2,1,0:T(8,128)(2,1)} custom-call(s32[3]{0:T(128)S(1)} %pad_add_fusion.pos, bf16[8,32,128]{2,1,0:T(8,128)(2,1)S(1)} %all_to_all.22.recv, bf16[8,96,128]{2,1,0:T(8,128)(2,1)S(1)} %get-tuple-element.21.low), custom_call_target="tpu_custom_call" | custom-call | bytes 655360 | tf_op jit(solution)/shard_map/pallas_call | solution.py:185
  72.5 3.5 %all-to-all-start.3 = ((bf16[8,192,128]{2,1,0:T(8,128)(2,1)}), bf16[8,192,128]{2,1,0:T(8,128)(2,1)S(1)}, u32[]{:S(2)}, u32[]{:S(2)}) async-start(bf16[8,192,128]{2,1,0:T(8,128)(2,1)} %shard_map.78), calls=%async_computation.3 | async-start | bytes 786432 | tf_op jit(solution)/shard_map/all_to_all | solution.py:197
  75.9 2.2 %shard_map.79 = (bf16[2,128,512]{2,1,0:T(8,128)(2,1)S(1)}, bf16[2,128,512]{2,1,0:T(8,128)(2,1)S(1)}, bf16[512,256]{1,0:T(8,128)(2,1)S(1)}, bf16[512,256]{1,0:T(8,128)(2,1)S(1)}) custom-call(bf16[3,512,256]{2,1,0:T(8,128)(2,1)S(1)} %get-tuple-element.18.qkv, bf16[512,256]{1,0:T(8,128)(2,1)S(1)} %copy-done, f32[2,16,512]{2,1,0:T(8,128)S(1)} %bitcast.6), custom_call_target="tpu_custom_call" | custom-call | flops 805306368 | bytes 2162688 | tf_op jit(solution)/shard_map/pallas_call | solution.py:185
  78.1 5.5 %all-to-all-done.3.recv_c = bf16[8,192,128]{2,1,0:T(8,128)(2,1)S(1)} async-done(((bf16[8,192,128]{2,1,0:T(8,128)(2,1)}), bf16[8,192,128]{2,1,0:T(8,128)(2,1)S(1)}, u32[]{:S(2)}, u32[]{:S(2)}) %all-to-all-start.3) | async-done | bytes 393248 | tf_op jit(solution)/shard_map/all_to_all | solution.py:197
  83.6 2.4 %shard_map.80 = (bf16[512,256]{1,0:T(8,128)(2,1)}, bf16[512,256]{1,0:T(8,128)(2,1)}, bf16[512,256]{1,0:T(8,128)(2,1)}, bf16[512,256]{1,0:T(8,128)(2,1)}) custom-call(s32[3]{0:T(128)S(1)} %pad_add_fusion.pos, bf16[3,512,256]{2,1,0:T(8,128)(2,1)S(1)} %get-tuple-element.18.qkv, bf16[512,256]{1,0:T(8,128)(2,1)S(1)} %copy-done, f32[2,16,512]{2,1,0:T(8,128)S(1)} %bitcast.7, ...), custom_call_target="tpu_custom_call" | custom-call | bytes 3604480 | tf_op jit(solution)/shard_map/pallas_call | solution.py:185
Async XLA Ops:
  0.6 21.4 %copy-start = (bf16[512,256]{1,0:T(8,128)(2,1)S(1)}, bf16[512,256]{1,0:T(8,128)(2,1)}, u32[]{:S(2)}) copy-start(bf16[512,256]{1,0:T(8,128)(2,1)} %g_in.3) | copy-start | bytes 786436
  0.6 21.4 %copy-start.1 = (f32[512,2,16]{0,2,1:T(8,128)S(1)}, f32[512,2,16]{0,2,1:T(8,128)}, u32[]{:S(2)}) copy-start(f32[512,2,16]{0,2,1:T(8,128)} %param.6) | copy-start | bytes 196612
  20.1 5.5 %collective-permute-start = (bf16[4,512,256]{2,1,0:T(8,128)(2,1)S(1)}, bf16[4,512,256]{2,1,0:T(8,128)(2,1)S(1)}, u32[]{:S(2)}, u32[]{:S(2)}) collective-permute-start(bf16[4,512,256]{2,1,0:T(8,128)(2,1)S(1)} %all_to_all.20.xa), channel_id=1, source_target_pairs={{0,1},{1,0},{2,3},{3,2},{4,5},{5,4},{6,7},{7,6},{8,9},{9,8},{10,11... | collective-permute-start | bytes 3145736 | tf_op jit(solution)/shard_map/ppermute | solution.py:207
  72.5 11.1 %all-to-all-start.3 = ((bf16[8,192,128]{2,1,0:T(8,128)(2,1)}), bf16[8,192,128]{2,1,0:T(8,128)(2,1)S(1)}, u32[]{:S(2)}, u32[]{:S(2)}) async-start(bf16[8,192,128]{2,1,0:T(8,128)(2,1)} %shard_map.78), calls=%async_computation.3 | async-start | bytes 786432 | tf_op jit(solution)/shard_map/all_to_all | solution.py:197

commit v3 on v2

--- a/solution.py
+++ b/solution.py
@@ -13,6 +13,7 @@
 NG = NX * NL
 NZ = 8
 NY = 4
+FIRST_Y, FIRST_P, FIRST_Z, FIRST_B = 2, 2, 4, 2
 Q = D // NG
 HQ = H * Q
 F32 = jnp.float32
@@ -49,7 +50,7 @@
         for j in range(6):
             row = lw[h, 10 + j : 11 + j, :] * level_scale(10 + j)
             g6[h, j * D : (j + 1) * D, :] = (g_t * row).astype(BF16)
-    rows = jnp.concatenate([xa[y] for y in range(NY)], 1)
+    rows = jnp.concatenate([xa[y ^ FIRST_Y] for y in range(NY)], 1)
     for c in range(3):
         copies[c].wait()
         part[c] = dot(rows, w_mine[c].reshape(NY * 256, 256))
@@ -58,7 +59,7 @@
 
 
 def project_kernel(xb, w_rest, part, g6, qkv, msg):
-    rows = jnp.concatenate([xb[y] for y in range(NY)], 1)
+    rows = jnp.concatenate([xb[y ^ FIRST_Y] for y in range(NY)], 1)
     for c in range(3):
         total = part[c] + dot(rows, w_rest[c].reshape(NY * 256, 256))
         qkv[c] = total.astype(BF16)
@@ -71,14 +72,14 @@
         for m, mat in enumerate(mats):
             at = m * HQ + h * Q
             for to in range(NG):
-                msg[to, at : at + Q, :] = mat[to * Q : (to + 1) * Q]
+                msg[to ^ FIRST_P, at : at + Q, :] = mat[to * Q : (to + 1) * Q]
 
 
 def spread_kernel(pos, recv, far, low, mats):
     z = pos[1]
 
     def total(m, sources):
-        terms = [recv[s, m * HQ : (m + 1) * HQ, :].astype(F32) for s in sources]
+        terms = [recv[s ^ FIRST_P, m * HQ : (m + 1) * HQ, :].astype(F32) for s in sources]
         return sum(terms[1:], terms[0])
 
     mats[0] = total(0, range(NG)).astype(BF16)
@@ -87,19 +88,19 @@
     for to in range(NZ):
         d = z ^ to
         top = (d >= 2).astype(jnp.int32) + (d >= 4).astype(jnp.int32)
-        far[to] = mats[jnp.where(to > z, 0, 1 + top)]
+        far[to ^ FIRST_Z] = mats[jnp.where(to > z, 0, 1 + top)]
     for j in range(3):
         for first in range(0, NG, 2**j):
             sent = total(1 + j if (first >> j) & 1 else 0, range(first, first + 2**j))
             for to in range(first ^ 2**j, (first ^ 2**j) + 2**j):
-                low[to, j * HQ : (j + 1) * HQ, :] = sent.astype(BF16)
+                low[to ^ FIRST_B, j * HQ : (j + 1) * HQ, :] = sent.astype(BF16)
 
 
 def collect_kernel(pos, recv, low, out):
     z = pos[1]
     out[:, : 3 * HQ, :] = low[...]
     for j in range(3):
-        first = lax.shift_left(lax.shift_right_logical(z, j) ^ 1, j)
+        first = lax.shift_left(lax.shift_right_logical(z ^ FIRST_Z, j) ^ 1, j)
         total = recv[first].astype(F32)
         for i in range(1, 2**j):
             total = total + recv[first + i].astype(F32)
@@ -151,7 +152,7 @@
         for j in range(6):
             at = j * HQ + h * Q
             slots.append(
-                jnp.concatenate([recv_c[src, at : at + Q, :].astype(F32) for src in range(NG)], 0)
+                jnp.concatenate([recv_c[src ^ FIRST_B, at : at + Q, :].astype(F32) for src in range(NG)], 0)
             )
         q_t, g_t = flipped(qkv[0, :, cols]), flipped(g_in[:, cols])
         later = jnp.zeros((D, D), F32)
@@ -193,8 +194,8 @@
     )(*head, *args)
 
 
-def swap(value, axis):
-    return lax.all_to_all(value, axis, 0, 0, tiled=True)
+def swap(value, axis, first):
+    return lax.all_to_all(value, axis, 0, 0, axis_index_groups=[[i ^ first for i in range(value.shape[0])]], tiled=True)
 
 
 def body(activations, w_proj, level_weight, g):
@@ -203,7 +204,7 @@
     lw = jnp.transpose(level_weight, (1, 2, 0))
     w = w_proj.reshape(3, NY, 2, 256, 256)
     half_flops = T * 1024 * 768 * 2
-    xa = swap(jnp.broadcast_to(activations[None], (NY, *activations.shape)), "y")
+    xa = swap(jnp.broadcast_to(activations[None], (NY, *activations.shape)), "y", FIRST_Y)
     xb = lax.ppermute(xa, "core", [(0, 1), (1, 0)])
     part, w_rest, g6 = call(
         half_kernel,
@@ -222,7 +223,7 @@
         (((3, T, H * D), BF16), ((NG, 7 * HQ, D), BF16)),
         flops=half_flops,
     )
-    recv_a = swap(msg, ("zl", "x"))
+    recv_a = swap(msg, ("zl", "x"), FIRST_P)
     far, low = call(
         spread_kernel,
         pos,
@@ -230,9 +231,9 @@
         (((NZ, HQ, D), BF16), ((NG, 3 * HQ, D), BF16)),
         [pltpu.VMEM((4, HQ, D), BF16)],
     )
-    recv_b = swap(far, "zh")
+    recv_b = swap(far, "zh", FIRST_Z)
     (back,) = call(collect_kernel, pos, (recv_b, low), (((NG, 6 * HQ, D), BF16),))
-    recv_c = swap(back, ("zl", "x"))
+    recv_c = swap(back, ("zl", "x"), FIRST_B)
     flat, tall = ((T, H * D), BF16), ((H, D, T), BF16)
     parts = call(
         attend_kernel,

time: 86.4 us -> 77.6 us (0.90)
  the two profiles are of different devices: /device:TPU:8 before, /device:TPU:16 now
where the time goes in v3:
time: 77.6 us; the launch traced here: 77.2 us
  blocking collectives  52.2 us (67%)
  Pallas kernels  12.1 us (16%)
  starting transfers between devices  7.91 us (10%)
  waiting for transfers between devices  3.18 us (4%)
  local copies, waits for them, and re-layouts  1.07 us (1%)
    all_to_all x3, blocking collectives, swap(): lax.all_to_all(value, axis, 0, 0, axis_index_groups=[[i ^ first for i in...  52.2 us
    pallas_call x6, Pallas kernels, call(): pl.pallas_call(kernel, out_shape=shapes, in_specs=[SMEM] * len(head) + [L...  12.1 us
    all_to_all x1, starting transfers between devices, swap(): lax.all_to_all(value, axis, 0, 0, axis_index_groups=[[i ^ first for i in...  6 us
    all_to_all x1, waiting for transfers between devices, swap(): lax.all_to_all(value, axis, 0, 0, axis_index_groups=[[i ^ first for i in...  3.18 us
    ppermute x1, starting transfers between devices, body(): xb = lax.ppermute(xa, 'core', [(0, 1), (1, 0)])  1.91 us
  transfers between devices with their start and end apart: 2, of which 1 were waited for; matrix products, arithmetic and copies ran while one was open for 0% of the time, Pallas kernels for 7%

profile of v3, /device:TPU:16, one launch (start us, length us, event | category | flops | bytes accessed | tf_op | source)
XLA Modules:
  0.0 77.2 jit_solution(311995686877251676)
XLA Ops:
  0.6 0.0 copy-start
  0.6 0.0 copy-start.1
  0.7 1.1 %broadcast_in_dim.2 = bf16[4,512,256]{2,1,0:T(8,128)(2,1)S(1)} broadcast(bf16[512,256]{1,0:T(8,128)(2,1)} %param.4), dimensions={1,2} | broadcast | bytes 1310720 | tf_op jit(solution)/shard_map/broadcast_in_dim | solution.py:207
  1.7 17.8 %all_to_all.20.xa = bf16[4,512,256]{2,1,0:T(8,128)(2,1)S(1)} all-to-all(bf16[4,512,256]{2,1,0:T(8,128)(2,1)S(1)} %broadcast_in_dim.2), channel_id=1, replica_groups={{4,6,0,2},{5,7,1,3},{12,14,8,10},{13,15,9,11},{20,22,16,18},{21,23,17,1..., dimensions={0} | all-to-all | bytes 2097152 | tf_op jit(solution)/shard_map/all_to_all | solution.py:198
  19.5 1.9 %collective-permute-start = (bf16[4,512,256]{2,1,0:T(8,128)(2,1)S(1)}, bf16[4,512,256]{2,1,0:T(8,128)(2,1)S(1)}, u32[]{:S(2)}, u32[]{:S(2)}) collective-permute-start(bf16[4,512,256]{2,1,0:T(8,128)(2,1)S(1)} %all_to_all.20.xa), channel_id=1, source_target_pairs={{0,1},{1,0},{2,3},{3,2},{4,5},{5,4},{6,7},{7,6},{8,9},{9,8},{10,11... | collective-permute-start | bytes 3145736 | tf_op jit(solution)/shard_map/ppermute | solution.py:208
  21.4 0.1 pad_add_fusion.pos
  21.5 0.0 copy-done
  21.5 0.0 copy-done.1
  21.5 3.5 %shard_map.75 = (f32[3,512,256]{2,1,0:T(8,128)S(1)}, bf16[3,4,256,256]{3,2,1,0:T(8,128)(2,1)S(1)}, bf16[2,768,512]{2,1,0:T(8,128)(2,1)S(1)}) custom-call(s32[3]{0:T(128)S(1)} %pad_add_fusion.pos, bf16[4,512,256]{2,1,0:T(8,128)(2,1)S(1)} %all_to_all.20.xa, bf16[3,4,2,256,256]{4,3,2,1,0:T(8,128)(2,1)} %bitcast.8, f32[2,16,512]{2,1,0:T(8,128)S(1)} %bitcast.5, ...), custom_call_target="tpu_custom_call" | custom-call | flops 805306368 | bytes 9240576 | tf_op jit(solution)/shard_map/pallas_call | solution.py:186
  25.0 0.0 collective-permute-done.xb
  25.0 2.2 %shard_map.76 = (bf16[3,512,256]{2,1,0:T(8,128)(2,1)S(1)}, bf16[8,224,128]{2,1,0:T(8,128)(2,1)S(1)}) custom-call(bf16[4,512,256]{2,1,0:T(8,128)(2,1)S(1)} %collective-permute-done.xb, bf16[3,4,256,256]{3,2,1,0:T(8,128)(2,1)S(1)} %get-tuple-element.15.w_rest, f32[3,512,256]{2,1,0:T(8,128)S(1)} %get-tuple-element.16.part, ...), custom_call_target="tpu_custom_call" | custom-call | flops 805306368 | bytes 7012352 | tf_op jit(solution)/shard_map/pallas_call | solution.py:186
  27.2 14.0 %all_to_all.21.recv = bf16[8,224,128]{2,1,0:T(8,128)(2,1)S(1)} all-to-all(bf16[8,224,128]{2,1,0:T(8,128)(2,1)S(1)} %get-tuple-element.19), channel_id=1, replica_groups={{16,24,0,8,48,56,32,40},{17,25,1,9,49,57,33,41},{18,26,2,10,50,58,34,42..., dimensions={0} | all-to-all | bytes 917504 | tf_op jit(solution)/shard_map/all_to_all | solution.py:198
  41.2 0.6 shard_map.77
  41.8 20.4 %all_to_all.22.recv = bf16[8,32,128]{2,1,0:T(8,128)(2,1)S(1)} all-to-all(bf16[8,32,128]{2,1,0:T(8,128)(2,1)S(1)} %get-tuple-element.20), channel_id=1, replica_groups={{256,320,384,448,0,64,128,192},{257,321,385,449,1,65,129,193},{258,322,..., dimensions={0} | all-to-all | bytes 131072 | tf_op jit(solution)/shard_map/all_to_all | solution.py:198
  62.2 1.3 %shard_map.78 = bf16[8,192,128]{2,1,0:T(8,128)(2,1)} custom-call(s32[3]{0:T(128)S(1)} %pad_add_fusion.pos, bf16[8,32,128]{2,1,0:T(8,128)(2,1)S(1)} %all_to_all.22.recv, bf16[8,96,128]{2,1,0:T(8,128)(2,1)S(1)} %get-tuple-element.21.low), custom_call_target="tpu_custom_call" | custom-call | bytes 655360 | tf_op jit(solution)/shard_map/pallas_call | solution.py:186
  63.5 6.0 %all-to-all-start.3 = ((bf16[8,192,128]{2,1,0:T(8,128)(2,1)}), bf16[8,192,128]{2,1,0:T(8,128)(2,1)S(1)}, u32[]{:S(2)}, u32[]{:S(2)}) async-start(bf16[8,192,128]{2,1,0:T(8,128)(2,1)} %shard_map.78), calls=%async_computation.3 | async-start | bytes 786432 | tf_op jit(solution)/shard_map/all_to_all | solution.py:198
  69.5 2.2 %shard_map.79 = (bf16[2,128,512]{2,1,0:T(8,128)(2,1)S(1)}, bf16[2,128,512]{2,1,0:T(8,128)(2,1)S(1)}, bf16[512,256]{1,0:T(8,128)(2,1)S(1)}, bf16[512,256]{1,0:T(8,128)(2,1)S(1)}) custom-call(bf16[3,512,256]{2,1,0:T(8,128)(2,1)S(1)} %get-tuple-element.18.qkv, bf16[512,256]{1,0:T(8,128)(2,1)S(1)} %copy-done, f32[2,16,512]{2,1,0:T(8,128)S(1)} %bitcast.6), custom_call_target="tpu_custom_call" | custom-call | flops 805306368 | bytes 2162688 | tf_op jit(solution)/shard_map/pallas_call | solution.py:186
  71.6 3.2 %all-to-all-done.3.recv_c = bf16[8,192,128]{2,1,0:T(8,128)(2,1)S(1)} async-done(((bf16[8,192,128]{2,1,0:T(8,128)(2,1)}), bf16[8,192,128]{2,1,0:T(8,128)(2,1)S(1)}, u32[]{:S(2)}, u32[]{:S(2)}) %all-to-all-start.3) | async-done | bytes 393248 | tf_op jit(solution)/shard_map/all_to_all | solution.py:198
  74.8 2.4 %shard_map.80 = (bf16[512,256]{1,0:T(8,128)(2,1)}, bf16[512,256]{1,0:T(8,128)(2,1)}, bf16[512,256]{1,0:T(8,128)(2,1)}, bf16[512,256]{1,0:T(8,128)(2,1)}) custom-call(s32[3]{0:T(128)S(1)} %pad_add_fusion.pos, bf16[3,512,256]{2,1,0:T(8,128)(2,1)S(1)} %get-tuple-element.18.qkv, bf16[512,256]{1,0:T(8,128)(2,1)S(1)} %copy-done, f32[2,16,512]{2,1,0:T(8,128)S(1)} %bitcast.7, ...), custom_call_target="tpu_custom_call" | custom-call | bytes 3604480 | tf_op jit(solution)/shard_map/pallas_call | solution.py:186
Async XLA Ops:
  0.6 20.9 %copy-start = (bf16[512,256]{1,0:T(8,128)(2,1)S(1)}, bf16[512,256]{1,0:T(8,128)(2,1)}, u32[]{:S(2)}) copy-start(bf16[512,256]{1,0:T(8,128)(2,1)} %g_in.3) | copy-start | bytes 786436
  0.6 20.9 %copy-start.1 = (f32[512,2,16]{0,2,1:T(8,128)S(1)}, f32[512,2,16]{0,2,1:T(8,128)}, u32[]{:S(2)}) copy-start(f32[512,2,16]{0,2,1:T(8,128)} %param.6) | copy-start | bytes 196612
  19.5 5.5 %collective-permute-start = (bf16[4,512,256]{2,1,0:T(8,128)(2,1)S(1)}, bf16[4,512,256]{2,1,0:T(8,128)(2,1)S(1)}, u32[]{:S(2)}, u32[]{:S(2)}) collective-permute-start(bf16[4,512,256]{2,1,0:T(8,128)(2,1)S(1)} %all_to_all.20.xa), channel_id=1, source_target_pairs={{0,1},{1,0},{2,3},{3,2},{4,5},{5,4},{6,7},{7,6},{8,9},{9,8},{10,11... | collective-permute-start | bytes 3145736 | tf_op jit(solution)/shard_map/ppermute | solution.py:208
  63.5 11.3 %all-to-all-start.3 = ((bf16[8,192,128]{2,1,0:T(8,128)(2,1)}), bf16[8,192,128]{2,1,0:T(8,128)(2,1)S(1)}, u32[]{:S(2)}, u32[]{:S(2)}) async-start(bf16[8,192,128]{2,1,0:T(8,128)(2,1)} %shard_map.78), calls=%async_computation.3 | async-start | bytes 786432 | tf_op jit(solution)/shard_map/all_to_all | solution.py:198
